TPU v7x, 256 devices: a whole 4x4x8 slice. The times are simulated.
256 devices in a mesh: half: 2 (over core), row: 8 (over z_hi, x), col: 16 (over y, z_lo).
Axes of the slice: x: 4, y: 4, z: 8 (z_hi: 2, z_lo: 4; z = z_hi * 4 + z_lo), core: 2. Of those that a mesh axis runs over, the one named last changes fastest.
Arguments:
- parent_front: float32 [16384, 16384], P(('half', 'row'), 'col'), may hold values from -6 to 6
- child_blocks: float32 [2, 8192, 8192], P('half', 'row', 'col'), may hold values from -6 to 6
- row_maps: int32 [2, 8192], replicated, may hold values from 0 to 16383, as said below
- inverse_blocks: float32 [4, 128, 128], replicated, may hold values from -0.12 to 0.12
Outputs:
- updated_front: float32 [16384, 16384], P(('half', 'row'), 'col')
- panel_factor: bfloat16 [16384, 512], P(('half', 'row'))
Inputs may be any that keep to these rules, and one draw needn't show every extreme that they name: `row_maps`: each row lists 8192 distinct parent rows. In every aligned block of 512 entries of a row, at most 64 entries fall in one aligned block of 1024 parent rows, and that bound is reached in every such block; in every aligned block of 1024 entries, at most 128 fall in one aligned block of 1024 parent rows, and that bound is reached in every such block.
All inputs are finite; a program needn't handle non-finite values.
Results may differ from a plain program's by a relative error of at most 0.001.
Values sent between devices are 32-bit elements; how exact they have to be, the bound alone decides.
A program may use at most 128 MiB of HBM per device.

v0:
```python
import jax
import jax.numpy as jnp
from jax import lax
from jax.sharding import PartitionSpec as P


def from_root(block, axis, holder):
    block = jnp.where(lax.axis_index(axis) == holder, block, jnp.zeros_like(block))
    return lax.psum(block, axis)


def highest_outer(left, right):
    return lax.dot_general(
        left,
        right,
        (((1,), (1,)), ((), ())),
        precision=lax.Precision.HIGHEST,
        preferred_element_type=jnp.float32,
    )


def ranks(targets, count):
    onehot = (targets[..., None] == jnp.arange(count, dtype=jnp.int32)).astype(jnp.int32)
    before = jnp.cumsum(onehot, axis=-2) - onehot
    return jnp.sum(before * onehot, axis=-1)


def row_tables(row_maps, row_loc, groups, cap_rows, my_group):
    parent_rows = row_maps.reshape(groups, -1)
    targets = parent_rows // row_loc
    slots = ranks(targets, groups)
    sources = jnp.arange(groups, dtype=jnp.int32)[:, None]
    where_at = jnp.where(targets == my_group, sources * cap_rows + slots, groups * cap_rows)
    table = (
        jnp.full((groups * cap_rows,), row_loc, jnp.int32)
        .at[where_at.reshape(-1)]
        .set((parent_rows % row_loc).reshape(-1), mode="drop")
    )
    send_at = targets[my_group] * cap_rows + slots[my_group]
    return (send_at, table)


def col_tables(row_maps, col_loc, n_col, cap_cols, my_col):
    parent_cols = row_maps.reshape(2, n_col, -1)
    targets = parent_cols // col_loc
    slots = ranks(targets, n_col)
    sources = jnp.arange(n_col, dtype=jnp.int32)[None, :, None]
    where_at = jnp.where(targets == my_col, sources * cap_cols + slots, n_col * cap_cols)
    child_index = jnp.broadcast_to(jnp.arange(2, dtype=jnp.int32)[:, None, None], where_at.shape)
    table = (
        jnp.full((2, n_col * cap_cols), col_loc, jnp.int32)
        .at[child_index, where_at]
        .set(parent_cols % col_loc, mode="drop")
    )
    send_at = targets[:, my_col] * cap_cols + slots[:, my_col]
    return (send_at, table)


def row_pack(values, send_at, total):
    return jnp.zeros((total, values.shape[1]), values.dtype).at[send_at].set(values)


def col_pack(values, send_at, total):
    return jnp.zeros((values.shape[0], total), values.dtype).at[:, send_at].set(values)


def local(parent_front, child_blocks, row_maps, inverse_blocks):
    row_loc, col_loc = parent_front.shape
    child_rows, child_cols = (child_blocks.shape[1], child_blocks.shape[2])
    n_row = lax.axis_size("row")
    n_col = lax.axis_size("col")
    groups = lax.axis_size("half") * n_row
    my_child = lax.axis_index("half")
    my_group = my_child * n_row + lax.axis_index("row")
    my_col = lax.axis_index("col")
    cap_cols = 2 * child_cols // n_col
    cap_rows = n_col // n_row * (child_cols // groups + child_cols // n_col)
    slab_rows = n_row * cap_rows
    row_send, row_table = row_tables(row_maps, row_loc, groups, cap_rows, my_group)
    col_send, col_table = col_tables(row_maps, col_loc, n_col, cap_cols, my_col)
    mine = child_blocks[0]
    moved = row_pack(mine, row_send, groups * cap_rows)
    arrived = lax.all_to_all(
        moved, ("half", "row"), split_axis=0, concat_axis=0, tiled=True
    ).reshape(2, slab_rows, child_cols)
    outgoing = jnp.stack(
        [col_pack(arrived[child], col_send[child], n_col * cap_cols) for child in range(2)]
    )
    landed = lax.all_to_all(outgoing, "col", split_axis=2, concat_axis=2, tiled=True)
    row_dest = row_table.reshape(2, slab_rows)
    assembled = parent_front
    for child in range(2):
        spread = (
            jnp.zeros((slab_rows, col_loc), jnp.float32)
            .at[:, col_table[child]]
            .add(landed[child], mode="drop")
        )
        assembled = assembled.at[row_dest[child]].add(spread, mode="drop")
    width = inverse_blocks.shape[1]
    count = inverse_blocks.shape[0]
    span = n_col // groups
    root = my_col // span
    factors = []
    tops = []
    for block in range(count):
        current = assembled[:, block * width : (block + 1) * width]
        if block > 0:
            earlier = jnp.concatenate(factors, axis=1)
            above = jnp.concatenate(
                [
                    tops[prior][(block - prior - 1) * width : (block - prior) * width]
                    for prior in range(block)
                ],
                axis=1,
            )
            current = current - highest_outer(earlier, above)
        result = highest_outer(current, jnp.tril(inverse_blocks[block]))
        factors.append(result)
        if block + 1 < count:
            tops.append(from_root(result[(block + 1) * width : count * width], ("half", "row"), 0))
    local_factor = jnp.concatenate(factors, axis=1)
    factor_rows = from_root(local_factor, "col", 0)
    factor_cols = from_root(factor_rows, ("half", "row"), root)
    updated_front = assembled - highest_outer(factor_rows, factor_cols)
    return (updated_front, factor_rows.astype(jnp.bfloat16))


def solution(mesh):
    in_specs = (P(("half", "row"), "col"), P("half", "row", "col"), P(), P())
    out_specs = (P(("half", "row"), "col"), P(("half", "row"), None))
    return jax.shard_map(local, mesh=mesh, in_specs=in_specs, out_specs=out_specs, check_vma=False)
```

profile of v0, /device:TPU:1, one launch (start us, length us, event | category | flops | bytes accessed | tf_op | source)
XLA Modules:
  0.0 1522.6 jit_solution(5224957147716496916)
XLA Ops:
  7.2 5.0 copy.95
  13.4 123.6 %reduce-window.14 = s32[16,16,8,128]{3,2,1,0:T(8,128)S(1)} reduce-window(s32[16,16,8,128]{3,2,1,0:T(8,128)} %fusion.34, s32[]{:T(128)} %constant.102.clone.1), window={size=1x1x1x128 pad=0_0x0_0x0_0x127_0}, to_apply=%region_0.1 | reduce-window | flops 33292288 | bytes 2097156 | tf_op jit(solution)/shard_map/reduce-window
  143.6 7.1 scatter_custom_fusion.1
  150.7 12.4 all-to-all-start
  163.5 36.3 %reduce-window.16 = s32[2,16,16,4,128]{4,2,3,1,0:T(8,128)S(1)} reduce-window(s32[2,16,16,4,128]{4,2,3,1,0:T(8,128)S(1)} %fusion.35, s32[]{:T(128)} %constant.102.clone.1), window={size=1x1x1x1x128 pad=0_0x0_0x0_0x0_0x127_0}, to_apply=%region_4.5 | reduce-window | flops 33292288 | bytes 2097156 | tf_op jit(solution)/shard_map/reduce-window.2
  201.9 59.7 %all-to-all-done = f32[16,128,512]{2,1,0:T(8,128)} async-done(((f32[16,128,512]{2,1,0:T(8,128)}), f32[16,128,512]{2,1,0:T(8,128)}, u32[]{:S(2)}, u32[]{:S(2)}) %all-to-all-start) | async-done | bytes 4194336 | tf_op jit(solution)/shard_map/all_to_all | solution.py:83
  261.6 4.2 fusion.82
  269.5 5.7 scatter_custom_fusion.2
  275.2 4.6 scatter_custom_fusion.3
  279.8 4.3 pad_maximum_fusion
  284.1 13.0 copy.34
  297.1 5.8 all-to-all-start.1
  303.7 60.3 %scatter_custom_fusion.8 = s32[2048]{0:T(1024)S(1)} fusion(s32[16384]{0:T(1024)S(1)} %bitcast.176, s32[16384]{0:T(1024)S(1)} %bitcast.177, s32[]{:T(128)} %constant.100.clone.1), kind=kCustom, calls=%fused_computation.152 | custom fusion | bytes 8196
  364.5 60.5 %scatter_custom_fusion = s32[2048]{0:T(1024)S(1)} fusion(s32[16384]{0:T(1024)S(1)} %bitcast.175, s32[16384]{0:T(1024)S(1)} %add_select_fusion.4, s32[]{:T(128)} %constant.100.clone.1), kind=kCustom, calls=%fused_computation.154 | custom fusion | bytes 8196 | tf_op jit(solution)/shard_map/scatter | solution.py:37
  425.0 63.9 %all-to-all-done.1 = f32[2,1024,1024]{1,0,2:T(2,128)} async-done(((f32[2,1024,1024]{1,0,2:T(2,128)}), f32[2,1024,1024]{1,0,2:T(2,128)}, u32[]{:S(2)}, u32[]{:S(2)}) %all-to-all-start.1) | async-done | bytes 8388640 | tf_op jit(solution)/shard_map/all_to_all | solution.py:89
  489.0 11.6 fusion.81
  500.5 13.6 scatter_custom_fusion.4
  514.1 5.3 copy.35
  519.5 14.0 scatter_custom_fusion.6
  533.4 5.3 copy.36
  538.8 14.4 scatter_fusion
  553.2 14.4 scatter_fusion.1
  570.3 174.1 %all-reduce.6.cloned.1.call-done = f32[384,128]{0,1:T(8,128)} async-done(((f32[384,128]{0,1:T(8,128)}), f32[384,128]{0,1:T(8,128)}) %all-reduce.6.cloned.1.call-update) | async-done | bytes 196624 | tf_op jit(solution)/shard_map/psum | solution.py:9
  744.4 2.1 convolution_subtract_fusion.2
  748.8 184.5 %all-reduce.8.cloned.1.call-done = f32[256,128]{0,1:T(8,128)} async-done(((f32[256,128]{0,1:T(8,128)}), f32[256,128]{0,1:T(8,128)}) %all-reduce.8.cloned.1.call-update) | async-done | bytes 131088 | tf_op jit(solution)/shard_map/psum | solution.py:9
  934.2 2.9 convolution_subtract_fusion.1
  938.6 177.9 %all-reduce.10.cloned.1.call-done = f32[128,128]{0,1:T(8,128)} async-done(((f32[128,128]{0,1:T(8,128)}), f32[128,128]{0,1:T(8,128)}) %all-reduce.10.cloned.1.call-update) | async-done | bytes 65552 | tf_op jit(solution)/shard_map/psum | solution.py:9
  1116.5 3.8 fusion.23
  1122.6 166.6 %all-reduce.12.cloned.1.call-done = f32[1024,512]{0,1:T(8,128)} async-done(((f32[1024,512]{0,1:T(8,128)}), f32[1024,512]{0,1:T(8,128)}) %all-reduce.12.cloned.1.call-update) | async-done | bytes 2097168 | tf_op jit(solution)/shard_map/psum | solution.py:9
  1289.2 4.1 fusion.83
  1294.6 210.5 %all-reduce.14.cloned.1.call-done = f32[1024,512]{0,1:T(8,128)} async-done(((f32[1024,512]{0,1:T(8,128)}), f32[1024,512]{0,1:T(8,128)}) %all-reduce.14.cloned.1.call-update) | async-done | bytes 2097168 | tf_op jit(solution)/shard_map/psum | solution.py:9
  1505.1 10.8 convolution_subtract_fusion
  (85 shorter events, 26.0 us)
Async XLA Ops:
  7.2 136.5 %copy-start = (f32[1,1024,512]{2,1,0:T(8,128)S(1)}, f32[1,1024,512]{2,1,0:T(8,128)}, u32[]{:S(2)}) copy-start(f32[1,1024,512]{2,1,0:T(8,128)} %param.5) | copy-start | bytes 6291460
  7.2 5.0 copy-start.2
  150.7 110.8 %all-to-all-start = ((f32[16,128,512]{2,1,0:T(8,128)}), f32[16,128,512]{2,1,0:T(8,128)}, u32[]{:S(2)}, u32[]{:S(2)}) async-start(f32[16,128,512]{2,1,0:T(8,128)} %bitcast.160), calls=%async_computation | async-start | bytes 8388608 | tf_op jit(solution)/shard_map/all_to_all | solution.py:83
  297.1 6.0 copy-start.5
  297.1 6.1 copy-start.4
  297.1 6.5 copy-start.3
  297.1 191.9 %all-to-all-start.1 = ((f32[2,1024,1024]{1,0,2:T(2,128)}), f32[2,1024,1024]{1,0,2:T(2,128)}, u32[]{:S(2)}, u32[]{:S(2)}) async-start(f32[2,1024,1024]{1,0,2:T(2,128)} %copy.34), calls=%async_computation.1 | async-start | bytes 16777216 | tf_op jit(solution)/shard_map/all_to_all | solution.py:89
  302.9 441.5 %all-reduce.6.cloned.1.call-start = ((), (), s32[]{:S(2)}) async-start(), calls=%async_computation.2 | async-start | bytes 393216 | tf_op jit(solution)/shard_map/psum | solution.py:9
  570.1 363.2 %all-reduce.8.cloned.1.call-start = ((), (), s32[]{:S(2)}) async-start(), calls=%async_computation.3 | async-start | bytes 262144 | tf_op jit(solution)/shard_map/psum | solution.py:9
  747.8 368.7 %all-reduce.10.cloned.1.call-start = ((), (), s32[]{:S(2)}) async-start(), calls=%async_computation.4 | async-start | bytes 131072 | tf_op jit(solution)/shard_map/psum | solution.py:9
  938.3 350.9 %all-reduce.12.cloned.1.call-start = ((), (), s32[]{:S(2)}) async-start(), calls=%async_computation.5 | async-start | bytes 4194304 | tf_op jit(solution)/shard_map/psum | solution.py:9
  1122.6 382.5 %all-reduce.14.cloned.1.call-start = ((), (), s32[]{:S(2)}) async-start(), calls=%async_computation.6 | async-start | bytes 4194304 | tf_op jit(solution)/shard_map/psum | solution.py:9
  1293.3 222.6 %copy-start.1 = (f32[1,1024,512]{2,1,0:T(8,128)S(1)}, f32[1,1024,512]{2,1,0:T(8,128)}, u32[]{:S(2)}) copy-start(f32[1,1024,512]{2,1,0:T(8,128)} %param.5) | copy-start | bytes 6291460
Sparse Core Ops, SparseCore 0:
  570.2 174.1 all-reduce.5
  748.0 185.2 all-reduce.7
  938.4 178.0 all-reduce.9
  1122.7 166.4 all-reduce.11
  1293.4 211.6 all-reduce.13
where the time goes:
time: 1540 us; the launch traced here: 1520 us
  waiting for transfers between devices  1040 us (68%)
  other arithmetic  233 us (15%)
  local copies, waits for them, and re-layouts  196 us (13%)
  matrix products  23.1 us (2%)
  starting transfers between devices  18.6 us (1%)
    psum x5, waiting for transfers between devices, from_root(): return lax.psum(block, axis)  913 us
    another operation x5, other arithmetic  161 us
    unnamed x24, local copies, waits for them, and re-layouts  67.2 us
    all_to_all x1, waiting for transfers between devices, local(): lax.all_to_all(outgoing, 'col', split_axis=2, concat_axis=2, tiled=True)  63.9 us
    scatter x1, local copies, waits for them, and re-layouts, row_tables(): table = jnp.full((groups * cap_rows,), row_loc, jnp.int32).at[where_at.re...  60.5 us
    all_to_all x1, waiting for transfers between devices, local(): lax.all_to_all(moved, ('half', 'row'), split_axis=0, concat_axis=0, tiled...  59.7 us
  transfers between devices with their start and end apart: 7, of which 7 were waited for; matrix products, arithmetic and copies ran while one was open for 11% of the time, Pallas kernels for 0%

commit v1 on v0

--- a/solution.py
+++ b/solution.py
@@ -86,7 +86,9 @@
     outgoing = jnp.stack(
         [col_pack(arrived[child], col_send[child], n_col * cap_cols) for child in range(2)]
     )
-    landed = lax.all_to_all(outgoing, "col", split_axis=2, concat_axis=2, tiled=True)
+    pieces = jnp.split(outgoing, lax.axis_size("col"), axis=2)
+    received = lax.all_to_all(jnp.stack(pieces), "col", 0, 0)
+    landed = jnp.concatenate(received, axis=2)
     row_dest = row_table.reshape(2, slab_rows)
     assembled = parent_front
     for child in range(2):

time: 1540 us -> 1530 us (level)
    unnamed x24 -> x28, local copies, waits for them, and re-layouts: 67.2 us -> 68.9 us
where the time goes in v1:
time: 1530 us; the launch traced here: 1520 us
  waiting for transfers between devices  1040 us (68%)
  other arithmetic  241 us (16%)
  local copies, waits for them, and re-layouts  182 us (12%)
  matrix products  23.1 us (2%)
  starting transfers between devices  18.7 us (1%)
    psum x5, waiting for transfers between devices, from_root(): return lax.psum(block, axis)  914 us
    another operation x5, other arithmetic  161 us
    unnamed x28, local copies, waits for them, and re-layouts  68.9 us
    all_to_all x1, waiting for transfers between devices, local(): received = lax.all_to_all(jnp.stack(pieces), 'col', 0, 0)  64.2 us
    scatter x1, local copies, waits for them, and re-layouts, row_tables(): table = jnp.full((groups * cap_rows,), row_loc, jnp.int32).at[where_at.re...  60.3 us
    all_to_all x1, waiting for transfers between devices, local(): lax.all_to_all(moved, ('half', 'row'), split_axis=0, concat_axis=0, tiled...  59.7 us
  transfers between devices with their start and end apart: 7, of which 7 were waited for; matrix products, arithmetic and copies ran while one was open for 11% of the time, Pallas kernels for 0%

profile of v1, /device:TPU:1, one launch (start us, length us, event | category | flops | bytes accessed | tf_op | source)
XLA Modules:
  0.0 1516.9 jit_solution(17354515607382744835)
XLA Ops:
  7.2 5.0 copy.85
  13.4 123.6 %reduce-window.14 = s32[16,16,8,128]{3,2,1,0:T(8,128)S(1)} reduce-window(s32[16,16,8,128]{3,2,1,0:T(8,128)} %fusion.30, s32[]{:T(128)} %constant.102.clone.1), window={size=1x1x1x128 pad=0_0x0_0x0_0x127_0}, to_apply=%region_0.1 | reduce-window | flops 33292288 | bytes 2097156 | tf_op jit(solution)/shard_map/reduce-window
  138.3 2.0 copy.13
  143.6 7.1 scatter_custom_fusion.1
  150.7 12.4 all-to-all-start
  163.5 36.3 %reduce-window.16 = s32[2,16,16,4,128]{4,2,3,1,0:T(8,128)S(1)} reduce-window(s32[2,16,16,4,128]{4,2,3,1,0:T(8,128)S(1)} %fusion.31, s32[]{:T(128)} %constant.102.clone.1), window={size=1x1x1x1x128 pad=0_0x0_0x0_0x0_0x127_0}, to_apply=%region_4.5 | reduce-window | flops 33292288 | bytes 2097156 | tf_op jit(solution)/shard_map/reduce-window.2
  201.9 59.7 %all-to-all-done = f32[16,128,512]{2,1,0:T(8,128)} async-done(((f32[16,128,512]{2,1,0:T(8,128)}), f32[16,128,512]{2,1,0:T(8,128)}, u32[]{:S(2)}, u32[]{:S(2)}) %all-to-all-start) | async-done | bytes 4194336 | tf_op jit(solution)/shard_map/all_to_all | solution.py:83
  261.6 4.2 fusion.95
  269.5 6.0 scatter_custom_fusion.2
  275.5 4.6 scatter_custom_fusion.3
  280.1 2.1 bitcast_dynamic-update-slice_fusion.14
  296.6 5.8 all-to-all-start.1
  303.2 60.3 %scatter_custom_fusion.8 = s32[2048]{0:T(1024)S(1)} fusion(s32[16384]{0:T(1024)S(1)} %bitcast.239, s32[16384]{0:T(1024)S(1)} %bitcast.240, s32[]{:T(128)} %constant.100.clone.1), kind=kCustom, calls=%fused_computation.210 | custom fusion | bytes 8196
  364.0 60.3 %scatter_custom_fusion = s32[2048]{0:T(1024)S(1)} fusion(s32[16384]{0:T(1024)S(1)} %bitcast.238, s32[16384]{0:T(1024)S(1)} %add_select_fusion.4, s32[]{:T(128)} %constant.100.clone.1), kind=kCustom, calls=%fused_computation.212 | custom fusion | bytes 8196 | tf_op jit(solution)/shard_map/scatter | solution.py:37
  424.4 64.2 %all-to-all-done.1 = f32[16,2,1024,64]{2,3,1,0:T(8,128)} async-done(((f32[16,2,1024,64]{2,3,1,0:T(8,128)}), f32[16,2,1024,64]{2,3,1,0:T(8,128)}, u32[]{:S(2)}, u32[]{:S(2)}) %all-to-all-start.1) | async-done | bytes 8388640 | tf_op jit(solution)/shard_map/all_to_all | solution.py:90
  488.5 8.4 fusion.94
  496.9 12.6 scatter_custom_fusion.6
  509.6 5.4 copy.21
  514.9 12.5 scatter_custom_fusion.4
  527.4 5.3 copy.20
  532.8 14.4 scatter_fusion
  547.2 14.4 scatter_fusion.1
  564.5 174.2 %all-reduce.6.cloned.1.call-done = f32[384,128]{0,1:T(8,128)} async-done(((f32[384,128]{0,1:T(8,128)}), f32[384,128]{0,1:T(8,128)}) %all-reduce.6.cloned.1.call-update) | async-done | bytes 196624 | tf_op jit(solution)/shard_map/psum | solution.py:9
  738.7 2.1 convolution_subtract_fusion.2
  743.1 184.5 %all-reduce.8.cloned.1.call-done = f32[256,128]{0,1:T(8,128)} async-done(((f32[256,128]{0,1:T(8,128)}), f32[256,128]{0,1:T(8,128)}) %all-reduce.8.cloned.1.call-update) | async-done | bytes 131088 | tf_op jit(solution)/shard_map/psum | solution.py:9
  928.5 2.9 convolution_subtract_fusion.1
  932.8 178.0 %all-reduce.10.cloned.1.call-done = f32[128,128]{0,1:T(8,128)} async-done(((f32[128,128]{0,1:T(8,128)}), f32[128,128]{0,1:T(8,128)}) %all-reduce.10.cloned.1.call-update) | async-done | bytes 65552 | tf_op jit(solution)/shard_map/psum | solution.py:9
  1110.7 3.8 fusion.19
  1116.9 166.6 %all-reduce.12.cloned.1.call-done = f32[1024,512]{0,1:T(8,128)} async-done(((f32[1024,512]{0,1:T(8,128)}), f32[1024,512]{0,1:T(8,128)}) %all-reduce.12.cloned.1.call-update) | async-done | bytes 2097168 | tf_op jit(solution)/shard_map/psum | solution.py:9
  1283.4 4.1 fusion.96
  1288.9 210.5 %all-reduce.14.cloned.1.call-done = f32[1024,512]{0,1:T(8,128)} async-done(((f32[1024,512]{0,1:T(8,128)}), f32[1024,512]{0,1:T(8,128)}) %all-reduce.14.cloned.1.call-update) | async-done | bytes 2097168 | tf_op jit(solution)/shard_map/psum | solution.py:9
  1499.3 10.8 convolution_subtract_fusion
  (103 shorter events, 38.4 us)
Async XLA Ops:
  7.2 136.5 %copy-start = (f32[1,1024,512]{2,1,0:T(8,128)S(1)}, f32[1,1024,512]{2,1,0:T(8,128)}, u32[]{:S(2)}) copy-start(f32[1,1024,512]{2,1,0:T(8,128)} %param.5) | copy-start | bytes 6291460
  7.2 5.0 copy-start.4
  150.7 110.8 %all-to-all-start = ((f32[16,128,512]{2,1,0:T(8,128)}), f32[16,128,512]{2,1,0:T(8,128)}, u32[]{:S(2)}, u32[]{:S(2)}) async-start(f32[16,128,512]{2,1,0:T(8,128)} %bitcast.223), calls=%async_computation | async-start | bytes 8388608 | tf_op jit(solution)/shard_map/all_to_all | solution.py:83
  280.1 2.5 copy-start.2
  280.1 3.8 copy-start.3
  296.6 6.0 copy-start.7
  296.6 6.1 copy-start.6
  296.6 6.5 copy-start.5
  296.6 191.9 %all-to-all-start.1 = ((f32[16,2,1024,64]{2,3,1,0:T(8,128)}), f32[16,2,1024,64]{2,3,1,0:T(8,128)}, u32[]{:S(2)}, u32[]{:S(2)}) async-start(f32[16,2,1024,64]{2,3,1,0:T(8,128)} %fusion.50), calls=%async_computation.1 | async-start | bytes 16777216 | tf_op jit(solution)/shard_map/all_to_all | solution.py:90
  302.4 436.3 %all-reduce.6.cloned.1.call-start = ((), (), s32[]{:S(2)}) async-start(), calls=%async_computation.2 | async-start | bytes 393216 | tf_op jit(solution)/shard_map/psum | solution.py:9
  564.1 363.5 %all-reduce.8.cloned.1.call-start = ((), (), s32[]{:S(2)}) async-start(), calls=%async_computation.3 | async-start | bytes 262144 | tf_op jit(solution)/shard_map/psum | solution.py:9
  742.1 368.6 %all-reduce.10.cloned.1.call-start = ((), (), s32[]{:S(2)}) async-start(), calls=%async_computation.4 | async-start | bytes 131072 | tf_op jit(solution)/shard_map/psum | solution.py:9
  932.6 350.8 %all-reduce.12.cloned.1.call-start = ((), (), s32[]{:S(2)}) async-start(), calls=%async_computation.5 | async-start | bytes 4194304 | tf_op jit(solution)/shard_map/psum | solution.py:9
  1116.8 382.5 %all-reduce.14.cloned.1.call-start = ((), (), s32[]{:S(2)}) async-start(), calls=%async_computation.6 | async-start | bytes 4194304 | tf_op jit(solution)/shard_map/psum | solution.py:9
  1287.5 222.6 %copy-start.1 = (f32[1,1024,512]{2,1,0:T(8,128)S(1)}, f32[1,1024,512]{2,1,0:T(8,128)}, u32[]{:S(2)}) copy-start(f32[1,1024,512]{2,1,0:T(8,128)} %param.5) | copy-start | bytes 6291460
Sparse Core Ops, SparseCore 0:
  564.2 174.5 all-reduce.5
  742.3 185.2 all-reduce.7
  932.7 177.9 all-reduce.9
  1116.9 166.4 all-reduce.11
  1287.6 211.6 all-reduce.13
